TPU v7x, 32 devices: a whole 2x2x4 slice. The times are simulated.
32 devices in a mesh: dp: 4 (over y, x), expert: 8 (over z, core).
Axes of the slice: x: 2, y: 2, z: 4, core: 2. Of those that a mesh axis runs over, the one named last changes fastest.
Arguments:
- inputs: bfloat16 [32768, 768], P(('dp', 'expert')), may hold values from -6 to 6
- cotangent: bfloat16 [32768, 768], P(('dp', 'expert')), may hold values from -6 to 6
- seq_group: int32 [32], P(('dp', 'expert')), may hold values from 0 to 7
- domain_counts: int32 [8], replicated, may hold values from 1 to 8
- sort_order: int32 [32, 1024], P(('dp', 'expert')), may hold values from 0 to 1023, each once within a row
- send_counts: int32 [32, 8], P(('dp', 'expert')), may hold values from 0 to 256, as said below
- gain_one: float32 [768], replicated, may hold values from 0.5 to 1.5
- shift_one: float32 [768], replicated, may hold values from -1.2 to 1.2
- gain_two: float32 [768], replicated, may hold values from 0.5 to 1.5
- shift_two: float32 [768], replicated, may hold values from -1.2 to 1.2
- w_query: bfloat16 [768, 768], replicated, may hold values from -0.3125 to 0.3125
- w_key: bfloat16 [768, 768], replicated, may hold values from -0.3125 to 0.3125
- w_value: bfloat16 [768, 768], replicated, may hold values from -0.21875 to 0.21875
- w_out: bfloat16 [768, 768], replicated, may hold values from -0.875 to 0.875
- router: bfloat16 [768, 8], replicated, may hold values from -0.15625 to 0.15625
- expert_in: bfloat16 [8, 768, 3072], P('expert'), may hold values from -0.21875 to 0.21875
- expert_out: bfloat16 [8, 3072, 768], P('expert'), may hold values from -0.3125 to 0.3125
Outputs:
- output: bfloat16 [32768, 768], P(('dp', 'expert'))
- grad_inputs: bfloat16 [32768, 768], P(('dp', 'expert'))
- grad_gain_one: float32 [768], replicated
- grad_shift_one: float32 [768], replicated
- grad_gain_two: float32 [768], replicated
- grad_shift_two: float32 [768], replicated
- grad_w_query: float32 [768, 768], replicated
- grad_w_key: float32 [768, 768], replicated
- grad_w_value: float32 [768, 768], replicated
- grad_w_out: float32 [768, 768], replicated
- grad_expert_in: float32 [8, 768, 3072], P('expert')
- grad_expert_out: float32 [8, 3072, 768], P('expert')
Inputs may be any that keep to these rules, and one draw needn't show every extreme that they name: `send_counts`: each row sums to 1024. One expert, the same in every row, gets exactly 256 tokens from every device; in each row one other expert gets none and the rest get between 64 and 192. `sort_order`: each row is a permutation of the local token indices.
All inputs are finite; a program needn't handle non-finite values.
Results may differ from a plain program's by a relative error of at most 0.015.
The roundings to bfloat16 on the way count: a program that leaves them out, or rounds other values in their place, can miss the bound.
Values may be sent and summed in bfloat16 or wider, within the bound.
A program may use at most 256 MiB of HBM per device.

v0:
```python
import jax
import jax.numpy as jnp
from jax import lax
from jax.sharding import PartitionSpec as P

HEADS = 12
HEAD_DIM = 64
LEN = 1024
epsilon = 1e-05


def layer_norm(values_in, scales, offsets):
    center = values_in - jnp.mean(values_in, axis=-1, keepdims=True)
    spread = jnp.mean(center * center, axis=-1, keepdims=True)
    return center * lax.rsqrt(spread + epsilon) * scales + offsets


def exact_gelu(pre_act):
    return jax.nn.gelu(pre_act, approximate=False)


def local(
    inputs,
    cotangent,
    seq_group,
    domain_counts,
    sort_order,
    send_counts,
    gain_one,
    shift_one,
    gain_two,
    shift_two,
    w_query,
    w_key,
    w_value,
    w_out,
    router,
    expert_in,
    expert_out,
):
    tok_rows, model_width = inputs.shape
    seq_count = tok_rows // LEN
    experts_total = send_counts.shape[1]
    capacity = 2 * tok_rows // experts_total
    senders = lax.axis_size("expert")
    scale_factor = HEAD_DIM ** (-0.5)
    counts_row = send_counts[0]
    count_ends = jnp.cumsum(counts_row)
    count_starts = count_ends - counts_row
    places = jnp.arange(tok_rows, dtype=jnp.int32)
    expert_ids = jnp.arange(experts_total, dtype=jnp.int32)
    expert_at = jnp.sum((places[:, None] >= count_ends[None, :]).astype(jnp.int32), axis=1)
    slot_at = places - jnp.sum(
        jnp.where(expert_at[:, None] == expert_ids[None, :], count_starts[None, :], 0), axis=1
    )
    dest_token = (
        jnp.zeros((tok_rows,), jnp.int32).at[sort_order[0]].set(expert_at * capacity + slot_at)
    )
    expert_token = jnp.zeros((tok_rows,), jnp.int32).at[sort_order[0]].set(expert_at)
    choose = (expert_token[:, None] == expert_ids[None, :]).astype(jnp.bfloat16)
    router_rows = jnp.einsum("te,de->td", choose, router, preferred_element_type=jnp.float32)
    inputs_f = inputs.astype(jnp.float32)
    normed_b = layer_norm(inputs_f, gain_one, shift_one).astype(jnp.bfloat16)
    query_rows = jnp.dot(normed_b, w_query, preferred_element_type=jnp.float32).astype(jnp.bfloat16)
    key_rows = jnp.dot(normed_b, w_key, preferred_element_type=jnp.float32).astype(jnp.bfloat16)
    value_rows = jnp.dot(normed_b, w_value, preferred_element_type=jnp.float32).astype(jnp.bfloat16)

    def heads_first(matrix):
        return matrix.reshape(seq_count, LEN, HEADS, HEAD_DIM).transpose(2, 0, 1, 3)

    def tokens_first(matrix):
        return matrix.transpose(1, 2, 0, 3).reshape(tok_rows, HEADS * HEAD_DIM)

    positions = jnp.arange(LEN, dtype=jnp.int32)
    causal = positions[:, None] >= positions[None, :]

    def head_scores(query_h, key_h):
        scores = (
            jnp.einsum("sqd,skd->sqk", query_h, key_h, preferred_element_type=jnp.float32)
            * scale_factor
        )
        return jnp.where(causal[None], scores, -1000000000.0)

    def head_forward(pieces):
        query_h, key_h, value_h = pieces
        scores = head_scores(query_h, key_h)
        row_peak = jnp.max(scores, axis=-1, keepdims=True)
        exp_scores = jnp.exp(scores - row_peak)
        row_total = jnp.sum(exp_scores, axis=-1, keepdims=True)
        attention = (exp_scores / row_total).astype(jnp.bfloat16)
        head_out = jnp.einsum(
            "sqk,skd->sqd", attention, value_h, preferred_element_type=jnp.float32
        )
        return (head_out.astype(jnp.bfloat16), (row_peak + jnp.log(row_total))[..., 0])

    query_heads = heads_first(query_rows)
    key_heads = heads_first(key_rows)
    value_heads = heads_first(value_rows)
    mixed_heads, log_totals = lax.map(head_forward, (query_heads, key_heads, value_heads))
    mixed_rows = tokens_first(mixed_heads)
    branch = jnp.dot(mixed_rows, w_out, preferred_element_type=jnp.float32)
    hidden = inputs_f + branch
    routed = layer_norm(hidden, gain_two, shift_two)
    routed_b = routed.astype(jnp.bfloat16)
    gate_vals = jax.nn.sigmoid(jnp.sum(routed * router_rows, axis=1))
    send_rows = (
        jnp.zeros((experts_total * capacity, model_width), jnp.bfloat16)
        .at[dest_token]
        .set(routed_b)
    )
    arrived = lax.all_to_all(
        send_rows.reshape(experts_total, capacity, model_width),
        "expert",
        split_axis=0,
        concat_axis=0,
        tiled=True,
    ).reshape(senders * capacity, model_width)
    first_weight = expert_in[0]
    second_weight = expert_out[0]
    pre_act = jnp.dot(arrived, first_weight, preferred_element_type=jnp.float32)
    act_rows = exact_gelu(pre_act).astype(jnp.bfloat16)
    expert_rows = jnp.dot(act_rows, second_weight, preferred_element_type=jnp.float32).astype(
        jnp.bfloat16
    )
    returned = lax.all_to_all(
        expert_rows.reshape(senders, capacity, model_width),
        "expert",
        split_axis=0,
        concat_axis=0,
        tiled=True,
    ).reshape(experts_total * capacity, model_width)
    back_rows = returned[dest_token].astype(jnp.float32)
    output = (hidden + gate_vals[:, None] * back_rows).astype(jnp.bfloat16)
    inverse = 1.0 / domain_counts.astype(jnp.float32)
    domain_weights = inverse / jnp.mean(inverse)
    domain_ids = jnp.arange(domain_counts.shape[0], dtype=jnp.int32)
    seq_weight = jnp.sum(
        jnp.where(seq_group[:, None] == domain_ids[None, :], domain_weights[None, :], 0.0), axis=1
    )
    grad_output = (
        cotangent.astype(jnp.float32).reshape(seq_count, LEN, model_width)
        * seq_weight[:, None, None]
    ).reshape(tok_rows, model_width)
    grad_back = (gate_vals[:, None] * grad_output).astype(jnp.bfloat16)
    grad_logit = jnp.sum(back_rows * grad_output, axis=1) * gate_vals * (1.0 - gate_vals)
    send_grads = (
        jnp.zeros((experts_total * capacity, model_width), jnp.bfloat16)
        .at[dest_token]
        .set(grad_back)
    )
    grad_arrived = lax.all_to_all(
        send_grads.reshape(experts_total, capacity, model_width),
        "expert",
        split_axis=0,
        concat_axis=0,
        tiled=True,
    ).reshape(senders * capacity, model_width)
    grad_act = jnp.einsum(
        "rd,fd->rf", grad_arrived, second_weight, preferred_element_type=jnp.float32
    )
    gelu_back = jax.vjp(exact_gelu, pre_act)[1]
    grad_pre = gelu_back(grad_act)[0].astype(jnp.bfloat16)
    grad_second = jnp.einsum(
        "rf,rd->fd", act_rows, grad_arrived, preferred_element_type=jnp.float32
    )
    grad_first = jnp.einsum("rd,rf->df", arrived, grad_pre, preferred_element_type=jnp.float32)
    grad_sent = jnp.einsum(
        "rf,df->rd", grad_pre, first_weight, preferred_element_type=jnp.float32
    ).astype(jnp.bfloat16)
    grad_returned = lax.all_to_all(
        grad_sent.reshape(senders, capacity, model_width),
        "expert",
        split_axis=0,
        concat_axis=0,
        tiled=True,
    ).reshape(experts_total * capacity, model_width)
    grad_routed = grad_returned[dest_token].astype(jnp.float32) + grad_logit[:, None] * router_rows
    norm_back_two = jax.vjp(layer_norm, hidden, gain_two, shift_two)[1]
    grad_hidden_norm, grad_gain_two, grad_shift_two = norm_back_two(grad_routed)
    grad_hidden = grad_output + grad_hidden_norm
    grad_branch = grad_hidden.astype(jnp.bfloat16)
    grad_w_out = jnp.einsum(
        "td,te->de", mixed_rows, grad_branch, preferred_element_type=jnp.float32
    )
    grad_mixed = jnp.einsum(
        "te,de->td", grad_branch, w_out, preferred_element_type=jnp.float32
    ).astype(jnp.bfloat16)

    def head_backward(pieces):
        query_h, key_h, value_h, grad_h, log_total = pieces
        attention = jnp.exp(head_scores(query_h, key_h) - log_total[..., None])
        attention_b = attention.astype(jnp.bfloat16)
        grad_value = jnp.einsum(
            "sqk,sqd->skd", attention_b, grad_h, preferred_element_type=jnp.float32
        )
        grad_attention = jnp.einsum(
            "sqd,skd->sqk", grad_h, value_h, preferred_element_type=jnp.float32
        )
        row_delta = jnp.sum(attention * grad_attention, axis=-1, keepdims=True)
        grad_scores = (attention * (grad_attention - row_delta)).astype(jnp.bfloat16)
        grad_query = (
            jnp.einsum("sqk,skd->sqd", grad_scores, key_h, preferred_element_type=jnp.float32)
            * scale_factor
        )
        grad_key = (
            jnp.einsum("sqk,sqd->skd", grad_scores, query_h, preferred_element_type=jnp.float32)
            * scale_factor
        )
        return (
            grad_query.astype(jnp.bfloat16),
            grad_key.astype(jnp.bfloat16),
            grad_value.astype(jnp.bfloat16),
        )

    grad_q_heads, grad_k_heads, grad_v_heads = lax.map(
        head_backward, (query_heads, key_heads, value_heads, heads_first(grad_mixed), log_totals)
    )
    grad_queries = tokens_first(grad_q_heads)
    grad_keys = tokens_first(grad_k_heads)
    grad_values = tokens_first(grad_v_heads)
    grad_w_query = jnp.einsum(
        "td,te->de", normed_b, grad_queries, preferred_element_type=jnp.float32
    )
    grad_w_key = jnp.einsum("td,te->de", normed_b, grad_keys, preferred_element_type=jnp.float32)
    grad_w_value = jnp.einsum(
        "td,te->de", normed_b, grad_values, preferred_element_type=jnp.float32
    )
    grad_normed = jnp.einsum("te,de->td", grad_queries, w_query, preferred_element_type=jnp.float32)
    grad_normed = grad_normed + jnp.einsum(
        "te,de->td", grad_keys, w_key, preferred_element_type=jnp.float32
    )
    grad_normed = grad_normed + jnp.einsum(
        "te,de->td", grad_values, w_value, preferred_element_type=jnp.float32
    )
    norm_back_one = jax.vjp(layer_norm, inputs_f, gain_one, shift_one)[1]
    grad_input_norm, grad_gain_one, grad_shift_one = norm_back_one(grad_normed)
    grad_inputs = (grad_hidden + grad_input_norm).astype(jnp.bfloat16)
    expert_sums = (
        lax.psum(grad_first.astype(jnp.bfloat16), "dp").astype(jnp.float32),
        lax.psum(grad_second.astype(jnp.bfloat16), "dp").astype(jnp.float32),
    )
    dense_sums = lax.psum(
        (
            grad_w_query,
            grad_w_key,
            grad_w_value,
            grad_w_out,
            grad_gain_one,
            grad_shift_one,
            grad_gain_two,
            grad_shift_two,
        ),
        ("dp", "expert"),
    )
    return (
        output,
        grad_inputs,
        dense_sums[4],
        dense_sums[5],
        dense_sums[6],
        dense_sums[7],
        dense_sums[0],
        dense_sums[1],
        dense_sums[2],
        dense_sums[3],
        expert_sums[0][None],
        expert_sums[1][None],
    )


def solution(mesh):
    return jax.shard_map(
        local,
        mesh=mesh,
        in_specs=(
            P(("dp", "expert"), None),
            P(("dp", "expert"), None),
            P(("dp", "expert")),
            P(),
            P(("dp", "expert"), None),
            P(("dp", "expert"), None),
            P(),
            P(),
            P(),
            P(),
            P(),
            P(),
            P(),
            P(),
            P(),
            P("expert", None, None),
            P("expert", None, None),
        ),
        out_specs=(
            P(("dp", "expert"), None),
            P(("dp", "expert"), None),
            P(),
            P(),
            P(),
            P(),
            P(),
            P(),
            P(),
            P(),
            P("expert", None, None),
            P("expert", None, None),
        ),
        check_vma=False,
    )
```

profile of v0, /device:TPU:0, one launch (start us, length us, event | category | flops | bytes accessed | tf_op | source)
XLA Modules:
  0.0 991.7 jit_solution(5724763379888539284)
XLA Ops:
  10.9 2.8 convolution_convert_fusion.4
  13.7 4.1 copy.59
  17.8 2.7 convolution_convert_fusion.3
  20.5 4.1 copy.60
  24.6 4.0 convolution_convert_fusion.5
  28.6 4.1 copy.58
  34.1 62.7 %while.28 = (s32[]{:T(128)}, bf16[12,1,1024,64]{2,3,1,0:T(8,128)(2,1)}, f32[12,1,1024]{2,1,0:T(1,128)}, bf16[12,1,1024,64]{3,2,1,0:T(8,128)(2,1)}, bf16[12,1,102...) while((s32[]{:T(128)}, bf16[12,1,1024,64]{2,3,1,0:T(8,128)(2,1)}, ...), condition=%wide.region_5.6_spmd.clone, body=%wide.region_2.5_spmd.clone.sunk | while | flops 284228608 | bytes 13544013 | solution.py:99
  96.7 3.3 fusion.123
  103.0 4.8 scatter_custom_fusion
  107.8 5.1 multiply_reduce_fusion.3
  114.6 4.3 scatter_custom_fusion.1
  119.6 7.9 scatter_custom_fusion.2
  127.5 78.0 %all_to_all.20 = bf16[8,256,768]{2,1,0:T(8,128)(2,1)S(1)} all-to-all(bf16[8,256,768]{2,1,0:T(8,128)(2,1)} %bitcast.180), channel_id=1, replica_groups=mesh['dp'=4,'expert'=8] {'expert'}, dimensions={0} | all-to-all | bytes 6291456 | tf_op jit(solution)/shard_map/all_to_all | solution.py:111
  205.5 63.5 %multiply_convert_fusion.1 = (bf16[2048,3072]{1,0:T(8,128)(2,1)S(1)}, f32[2048,3072]{1,0:T(8,128)}, f32[2048,3072]{1,0:T(8,128)}) fusion(bf16[2048,768]{1,0:T(8,128)(2,1)S(1)} %bitcast.185, bf16[1,768,3072]{2,1,0:T(8,128)(2,1)} %param.36), kind=kOutput, calls=%fused_computation.72 | convolution fusion | flops 10072621056 | bytes 70778880 | tf_op jit(solution)/shard_map/dot_general | solution.py:120
  269.0 11.2 %fusion.82 = bf16[2048,768]{1,0:T(8,128)(2,1)} fusion(bf16[2048,3072]{1,0:T(8,128)(2,1)S(1)} %get-tuple-element.228, bf16[1,3072,768]{2,1,0:T(8,128)(2,1)S(1)} %copy-done.42), kind=kOutput, calls=%fused_computation.111 | convolution fusion | flops 9665249280 | bytes 20447232 | tf_op jit(solution)/shard_map/dot_general | solution.py:122
  280.2 4.7 all-to-all-start.1
  289.3 67.2 %all-to-all-done.1 = bf16[8,256,768]{2,1,0:T(8,128)(2,1)} async-done(((bf16[8,256,768]{2,1,0:T(8,128)(2,1)}), bf16[8,256,768]{2,1,0:T(8,128)(2,1)}, u32[]{:S(2)}, u32[]{:S(2)}) %all-to-all-start.1) | async-done | bytes 3145760 | tf_op jit(solution)/shard_map/all_to_all | solution.py:125
  356.5 7.9 gather_fusion
  364.3 2.6 copy.62
  366.9 4.0 multiply_convert_fusion.2
  370.9 2.6 copy.64
  373.4 7.9 scatter_custom_fusion.3
  381.3 76.2 %all_to_all.21 = bf16[8,256,768]{2,1,0:T(8,128)(2,1)} all-to-all(bf16[8,256,768]{2,1,0:T(8,128)(2,1)} %bitcast.179), channel_id=1, replica_groups=mesh['dp'=4,'expert'=8] {'expert'}, dimensions={0} | all-to-all | bytes 6291456 | tf_op jit(solution)/shard_map/all_to_all | solution.py:151
  457.6 32.8 %add_convert_fusion = bf16[2048,3072]{1,0:T(8,128)(2,1)} fusion(f32[2048,3072]{1,0:T(8,128)} %get-tuple-element.229, f32[2048,3072]{1,0:T(8,128)} %get-tuple-element.244, bf16[2048,768]{1,0:T(8,128)(2,1)} %bitcast.188, bf16[1,3072,768]{2,1,0:T(8,128)(2,1)} %param.37), kind=kOutput, calls=%fused_computation.71 | convolution fusion | flops 9751756800 | bytes 70778880 | tf_op jit(solution)/shard_map/rd,fd->rf/dot_general | solution.py:158
  490.4 15.4 %fusion.79 = bf16[2048,768]{1,0:T(8,128)(2,1)} fusion(bf16[2048,3072]{1,0:T(8,128)(2,1)} %add_convert_fusion, bf16[1,768,3072]{2,1,0:T(8,128)(2,1)} %param.36), kind=kOutput, calls=%fused_computation.110 | convolution fusion | flops 9665249280 | bytes 20447232 | tf_op jit(solution)/shard_map/rf,df->rd/dot_general | solution.py:167
  505.8 4.4 all-to-all-start.3
  510.8 15.5 %fusion.76 = bf16[1,3072,768]{2,1,0:T(8,128)(2,1)} fusion(bf16[2048,3072]{1,0:T(8,128)(2,1)} %copy-done.49, bf16[2048,768]{1,0:T(8,128)(2,1)} %bitcast.189), kind=kOutput, calls=%fused_computation.105 | convolution fusion | flops 9666035712 | bytes 20447232 | tf_op jit(solution)/shard_map/rf,rd->fd/dot_general | solution.py:163
  526.4 14.5 %fusion.75 = bf16[1,768,3072]{2,1,0:T(8,128)(2,1)} fusion(bf16[2048,768]{1,0:T(8,128)(2,1)S(1)} %bitcast.186, bf16[2048,3072]{1,0:T(8,128)(2,1)} %add_convert_fusion), kind=kOutput, calls=%fused_computation.104 | convolution fusion | flops 9666035712 | bytes 20447232 | tf_op jit(solution)/shard_map/rd,rf->df/dot_general | solution.py:166
  541.1 40.7 %all-to-all-done.3 = bf16[8,256,768]{2,1,0:T(8,128)(2,1)} async-done(((bf16[8,256,768]{2,1,0:T(8,128)(2,1)}), bf16[8,256,768]{2,1,0:T(8,128)(2,1)}, u32[]{:S(2)}, u32[]{:S(2)}) %all-to-all-start.3) | async-done | bytes 3145760 | tf_op jit(solution)/shard_map/all_to_all | solution.py:170
  581.8 7.9 gather_fusion.1
  589.7 2.6 copy.65
  592.4 4.9 multiply_reduce_fusion.1
  598.0 3.9 fusion.121
  605.6 2.8 copy.66
  612.5 151.5 %while.29 = (s32[]{:T(128)}, bf16[12,1,1024,64]{2,3,1,0:T(8,128)(2,1)}, bf16[12,1,1024,64]{2,3,1,0:T(8,128)(2,1)}, bf16[12,1,1024,64]{2,3,1,0:T(8,128)(2,1)}, bf...) while((s32[]{:T(128)}, ...), condition=%wide.region_23.24_spmd.clone, body=%wide.region_21.23_spmd.clone.sunk | while | flops 681901056 | bytes 33711208 | solution.py:215
  618.2 2.4 fusion.186
  635.3 2.4 fusion.187
  643.3 2.4 fusion.186
  647.9 2.4 fusion.187
  656.0 2.4 fusion.186
  660.6 2.4 fusion.187
  668.6 2.4 fusion.186
  681.3 2.4 fusion.186
  685.9 2.4 fusion.187
  694.0 2.4 fusion.186
  698.5 2.4 fusion.187
  706.6 2.4 fusion.186
  711.2 2.4 fusion.187
  731.8 2.4 fusion.186
  756.9 2.4 fusion.186
  764.1 4.8 fusion.124
  769.0 4.4 fusion.111
  773.4 4.4 fusion.113
  777.8 4.4 fusion.115
  782.3 3.2 fusion.125
  785.6 2.8 fusion.126
  788.4 3.4 fusion.120
  794.3 3.5 add_convert_fusion.1
  797.8 2.7 copy.71
  802.1 40.3 %all-reduce = (f32[768]{0:T(1024)}, f32[768]{0:T(1024)}, f32[768]{0:T(1024)}, f32[768]{0:T(1024)}) all-reduce(f32[768]{0:T(1024)S(1)} %get-tuple-element.181, f32[768]{0:T(1024)S(1)} %get-tuple-element.184, f32[768]{0:T(1024)S(1)} %get-tuple-element.179, ...), channel_id=1, replica_groups=mesh['dp'=4,'expert'=8] {'dp','expert'}, use_global_device_ids=true, to_apply=%region_27.28 | all-reduce | flops 3072 | bytes 24576 | tf_op jit(solution)/shard_map/psum | solution.py:242
  842.4 7.5 broadcast_in_dim.122
  849.9 4.5 broadcast_in_dim.124
  854.4 120.3 %all-reduce.6.cloned.1.call-done = (f32[768,768]{1,0:T(8,128)}, f32[768,768]{1,0:T(8,128)}, f32[768,768]{1,0:T(8,128)}, f32[768,768]{1,0:T(8,128)}) async-done(((f32[768,768]{1,0:T(8,128)}, f32[768,768]{1,0:T(8,128)}, f32[768,768]{1,0:T(8,128)}, f32[768,768]{1,0:T(8,128)}), (f32[768,768]{1,0:T(8,128)}, f32[768,768]{1,0:T(8,128)}, f32[768,768]{1,0:T(8,128)}, ...) | async-done | bytes 9437200 | tf_op jit(solution)/shard_map/psum | solution.py:242
  974.6 3.4 copy.112
  (271 shorter events, 210.7 us)
Async XLA Ops:
  7.2 10.6 %copy-start = (bf16[768,768]{1,0:T(8,128)(2,1)S(1)}, bf16[768,768]{1,0:T(8,128)(2,1)}, u32[]{:S(2)}) copy-start(bf16[768,768]{1,0:T(8,128)(2,1)} %param.33) | copy-start | bytes 3538948
  7.2 3.2 copy-start.28
  7.2 3.2 copy-start.46
  9.0 87.7 %copy-start.1 = (bf16[1024,768]{0,1:T(8,128)(2,1)}, bf16[1024,768]{0,1:T(8,128)(2,1)S(1)}, u32[]{:S(2)}) copy-start(bf16[1024,768]{0,1:T(8,128)(2,1)S(1)} %copy.57) | copy-start | bytes 4718596
  9.0 1.8 copy-start.44
  9.3 15.3 %copy-start.21 = (f32[1024]{0:T(1024)}, f32[1024]{0:T(1024)S(1)}, u32[]{:S(2)}) copy-start(f32[1024]{0:T(1024)S(1)} %broadcast_multiply_fusion.1) | copy-start | bytes 12292
  9.8 0.6 copy-start.32
  10.9 13.7 %copy-start.30 = (f32[1024]{0:T(1024)}, f32[1024]{0:T(1024)S(1)}, u32[]{:S(2)}) copy-start(f32[1024]{0:T(1024)S(1)} %fusion.102) | copy-start | bytes 12292
  100.0 1.7 copy-start.3
  100.0 2.6 copy-start.48
  100.0 2.9 copy-start.40
  100.0 7.8 copy-start.25
  100.1 7.8 copy-start.37
  100.1 7.8 copy-start.38
  100.1 12.9 %copy-start.19 = (f32[1024]{0:T(1024)}, f32[1024]{0:T(1024)S(1)}, u32[]{:S(2)}) copy-start(f32[1024]{0:T(1024)S(1)} %broadcast_multiply_fusion) | copy-start | bytes 12292
  102.1 0.6 copy-start.34
  102.7 10.3 %copy-start.23 = (f32[1024]{0:T(1024)}, f32[1024]{0:T(1024)S(1)}, u32[]{:S(2)}) copy-start(f32[1024]{0:T(1024)S(1)} %fusion.103) | copy-start | bytes 12292
  119.6 85.9 %copy-start.39 = (s32[1024]{0:T(1024)}, s32[1024]{0:T(1024)S(1)}, u32[]{:S(2)}) copy-start(s32[1024]{0:T(1024)S(1)} %get-tuple-element.240) | copy-start | bytes 12292
  205.5 63.5 %copy-start.13 = (bf16[8,256,768]{2,1,0:T(8,128)(2,1)}, bf16[8,256,768]{2,1,0:T(8,128)(2,1)S(1)}, u32[]{:S(2)}) copy-start(bf16[8,256,768]{2,1,0:T(8,128)(2,1)S(1)} %all_to_all.20) | copy-start | bytes 9437188
  205.5 63.5 %copy-start.42 = (bf16[1,3072,768]{2,1,0:T(8,128)(2,1)S(1)}, bf16[1,3072,768]{2,1,0:T(8,128)(2,1)}, u32[]{:S(2)}) copy-start(bf16[1,3072,768]{2,1,0:T(8,128)(2,1)} %param.37) | copy-start | bytes 14155780
  269.0 11.3 %copy-start.49 = (bf16[2048,3072]{1,0:T(8,128)(2,1)}, bf16[2048,3072]{1,0:T(8,128)(2,1)S(1)}, u32[]{:S(2)}) copy-start(bf16[2048,3072]{1,0:T(8,128)(2,1)S(1)} %get-tuple-element.228) | copy-start | bytes 37748740
  280.2 76.2 %all-to-all-start.1 = ((bf16[8,256,768]{2,1,0:T(8,128)(2,1)}), bf16[8,256,768]{2,1,0:T(8,128)(2,1)}, u32[]{:S(2)}, u32[]{:S(2)}) async-start(bf16[8,256,768]{2,1,0:T(8,128)(2,1)} %bitcast.190), calls=%async_computation.1 | async-start | bytes 6291456 | tf_op jit(solution)/shard_map/all_to_all | solution.py:125
  284.9 2.4 copy-start.41
  284.9 4.4 copy-start.27
  285.0 71.5 %copy-start.36 = (s32[1024]{0:T(1024)S(1)}, s32[1024]{0:T(1024)}, u32[]{:S(2)}) copy-start(s32[1024]{0:T(1024)} %get-tuple-element.239) | copy-start | bytes 12292
  286.7 315.3 %copy-start.8 = (bf16[1024,768]{0,1:T(8,128)(2,1)}, bf16[1024,768]{0,1:T(8,128)(2,1)S(1)}, u32[]{:S(2)}) copy-start(bf16[1024,768]{0,1:T(8,128)(2,1)S(1)} %copy.63) | copy-start | bytes 4718596
  505.8 76.0 %all-to-all-start.3 = ((bf16[8,256,768]{2,1,0:T(8,128)(2,1)}), bf16[8,256,768]{2,1,0:T(8,128)(2,1)}, u32[]{:S(2)}, u32[]{:S(2)}) async-start(bf16[8,256,768]{2,1,0:T(8,128)(2,1)} %bitcast.187), calls=%async_computation.3 | async-start | bytes 6291456 | tf_op jit(solution)/shard_map/all_to_all | solution.py:170
  510.3 332.1 %all-reduce.8.cloned.1.call-start = ((), (), s32[]{:S(2)}) async-start(), calls=%async_computation.5 | async-start | bytes 18874368 | tf_op jit(solution)/shard_map/psum | solution.py:239
  510.8 15.6 %copy-start.14 = (bf16[8,256,768]{2,1,0:T(8,128)(2,1)S(1)}, bf16[8,256,768]{2,1,0:T(8,128)(2,1)}, u32[]{:S(2)}) copy-start(bf16[8,256,768]{2,1,0:T(8,128)(2,1)} %copy-done.13) | copy-start | bytes 9437188
  540.9 433.8 %all-reduce.6.cloned.1.call-start = ((), (), s32[]{:S(2)}) async-start(), calls=%async_computation.4 | async-start | bytes 18874368 | tf_op jit(solution)/shard_map/psum | solution.py:242
  589.7 2.6 copy-start.20
  589.7 2.6 copy-start.24
  589.7 2.6 copy-start.26
  592.3 5.0 copy-start.35
  592.3 5.0 copy-start.4
  592.3 5.3 copy-start.5
  592.4 5.7 copy-start.10
  602.0 1.6 copy-start.6
  602.0 2.2 copy-start.43
  604.2 1.4 copy-start.18
  764.0 4.9 copy-start.2
  764.1 4.9 copy-start.22
  764.1 4.9 copy-start.29
  764.1 4.9 copy-start.31
  764.1 4.9 copy-start.47
  782.3 3.3 copy-start.45
  788.4 3.4 copy-start.33
  791.8 2.0 copy-start.7
  791.8 2.5 copy-start.9
  797.8 2.7 copy-start.11
  842.4 7.5 copy-start.12
  974.6 3.4 copy-start.17
  978.0 2.5 copy-start.16
  980.5 2.5 copy-start.15
Sparse Core Ops, SparseCore 0:
  541.0 190.5 all-reduce.7
  782.4 192.1 all-reduce.5
where the time goes:
time: 1000 us; the launch traced here: 992 us
  matrix products  378 us (38%)
  waiting for transfers between devices  228 us (23%)
  blocking collectives  195 us (20%)
  local copies, waits for them, and re-layouts  110 us (11%)
  other arithmetic  54.5 us (5%)
  between operations  16.4 us (2%)
    psum x1, waiting for transfers between devices, local(): lax.psum((grad_w_query, grad_w_key, grad_w_value, grad_w_out, grad_gain_o...  120 us
    all_to_all x1, blocking collectives, local(): lax.all_to_all(send_rows.reshape(experts_total, capacity, model_width), '...  78 us
    all_to_all x1, blocking collectives, local(): lax.all_to_all(send_grads.reshape(experts_total, capacity, model_width),...  76.2 us
    all_to_all x1, waiting for transfers between devices, local(): lax.all_to_all(expert_rows.reshape(senders, capacity, model_width), 'expe...  67.2 us
    dot_general x1, matrix products, local(): pre_act = jnp.dot(arrived, first_weight, preferred_element_type=jnp.float32)  63.5 us
    dot_general x24, matrix products, head_scores(): jnp.einsum('sqd,skd->sqk', query_h, key_h, preferred_element_type=jnp.flo...  46.3 us
    all_to_all x1, waiting for transfers between devices, local(): lax.all_to_all(grad_sent.reshape(senders, capacity, model_width), 'expert...  40.7 us
    psum x1, blocking collectives, local(): lax.psum((grad_w_query, grad_w_key, grad_w_value, grad_w_out, grad_gain_o...  40.3 us
  transfers between devices with their start and end apart: 4, of which 3 were waited for; matrix products, arithmetic and copies ran while one was open for 26% of the time, Pallas kernels for 0%

commit v1 on v0

--- a/solution.py
+++ b/solution.py
@@ -239,7 +239,7 @@
         lax.psum(grad_first.astype(jnp.bfloat16), "dp").astype(jnp.float32),
         lax.psum(grad_second.astype(jnp.bfloat16), "dp").astype(jnp.float32),
     )
-    dense_sums = lax.psum(
+    inner = lax.psum(
         (
             grad_w_query,
             grad_w_key,
@@ -250,8 +250,9 @@
             grad_gain_two,
             grad_shift_two,
         ),
-        ("dp", "expert"),
-    )
+        "expert",
+    )
+    dense_sums = lax.psum(inner, "dp")
     return (
         output,
         grad_inputs,

time: 1000 us -> 1390 us (1.39)
  waiting for transfers between devices: 228 us -> 616 us
    psum x0 -> x1, waiting for transfers between devices: none -> 182 us  [local(): dense_sums = lax.psum(inner, 'dp')]
    psum x1, waiting for transfers between devices: 0.01 us -> 131 us  [local(): lax.psum(grad_first.astype(jnp.bfloat16), 'dp').astype(jnp.float32)]
    psum x1, waiting for transfers between devices: 120 us -> 165 us  [local(): lax.psum((grad_w_query, grad_w_key, grad_w_value, grad_w_out, grad_gain_o...]
    all_to_all x1, waiting for transfers between devices: 40.7 us -> 71 us  [local(): lax.all_to_all(grad_sent.reshape(senders, capacity, model_width), 'expert...]
    psum x0 -> x1, blocking collectives: none -> 17 us  [local(): dense_sums = lax.psum(inner, 'dp')]
  transfers between devices with their start and end apart: 4 -> 5, of which waited for: 3 -> 5; matrix products, arithmetic and copies ran while one was open for 26% -> 5% of each run, Pallas kernels for 0% -> 0%
where the time goes in v1:
time: 1390 us; the launch traced here: 1380 us
  waiting for transfers between devices  616 us (44%)
  matrix products  373 us (27%)
  blocking collectives  198 us (14%)
  local copies, waits for them, and re-layouts  109 us (8%)
  other arithmetic  54.5 us (4%)
  between operations  15.9 us (1%)
    psum x1, waiting for transfers between devices, local(): dense_sums = lax.psum(inner, 'dp')  182 us
    psum x1, waiting for transfers between devices, local(): lax.psum((grad_w_query, grad_w_key, grad_w_value, grad_w_out, grad_gain_o...  165 us
    psum x1, waiting for transfers between devices, local(): lax.psum(grad_first.astype(jnp.bfloat16), 'dp').astype(jnp.float32)  131 us
    all_to_all x1, blocking collectives, local(): lax.all_to_all(send_rows.reshape(experts_total, capacity, model_width), '...  78 us
    all_to_all x1, blocking collectives, local(): lax.all_to_all(send_grads.reshape(experts_total, capacity, model_width),...  76.2 us
    all_to_all x1, waiting for transfers between devices, local(): lax.all_to_all(grad_sent.reshape(senders, capacity, model_width), 'expert...  71 us
    all_to_all x1, waiting for transfers between devices, local(): lax.all_to_all(expert_rows.reshape(senders, capacity, model_width), 'expe...  67.2 us
    dot_general x1, matrix products, local(): pre_act = jnp.dot(arrived, first_weight, preferred_element_type=jnp.float32)  63.5 us
  transfers between devices with their start and end apart: 5, of which 5 were waited for; matrix products, arithmetic and copies ran while one was open for 5% of the time, Pallas kernels for 0%

profile of v1, /device:TPU:0, one launch (start us, length us, event | category | flops | bytes accessed | tf_op | source)
XLA Modules:
  0.0 1377.5 jit_solution(715133831639086327)
XLA Ops:
  10.9 2.8 convolution_convert_fusion.4
  13.7 4.1 copy.59
  17.8 2.7 convolution_convert_fusion.3
  20.5 4.1 copy.60
  24.6 4.0 convolution_convert_fusion.5
  28.6 4.1 copy.58
  34.1 62.7 %while.28 = (s32[]{:T(128)}, bf16[12,1,1024,64]{2,3,1,0:T(8,128)(2,1)}, f32[12,1,1024]{2,1,0:T(1,128)}, bf16[12,1,1024,64]{3,2,1,0:T(8,128)(2,1)}, bf16[12,1,102...) while((s32[]{:T(128)}, bf16[12,1,1024,64]{2,3,1,0:T(8,128)(2,1)}, ...), condition=%wide.region_5.6_spmd.clone, body=%wide.region_2.5_spmd.clone.sunk | while | flops 284228608 | bytes 13544013 | solution.py:99
  96.7 3.3 fusion.123
  102.6 4.8 scatter_custom_fusion
  107.5 5.1 multiply_reduce_fusion.3
  114.3 4.3 scatter_custom_fusion.1
  119.2 8.0 scatter_custom_fusion.2
  127.2 78.0 %all_to_all.20 = bf16[8,256,768]{2,1,0:T(8,128)(2,1)S(1)} all-to-all(bf16[8,256,768]{2,1,0:T(8,128)(2,1)} %bitcast.180), channel_id=1, replica_groups=mesh['dp'=4,'expert'=8] {'expert'}, dimensions={0} | all-to-all | bytes 6291456 | tf_op jit(solution)/shard_map/all_to_all | solution.py:111
  205.2 63.5 %multiply_convert_fusion.1 = (bf16[2048,3072]{1,0:T(8,128)(2,1)S(1)}, f32[2048,3072]{1,0:T(8,128)}, f32[2048,3072]{1,0:T(8,128)}) fusion(bf16[2048,768]{1,0:T(8,128)(2,1)S(1)} %bitcast.185, bf16[1,768,3072]{2,1,0:T(8,128)(2,1)} %param.36), kind=kOutput, calls=%fused_computation.72 | convolution fusion | flops 10072621056 | bytes 70778880 | tf_op jit(solution)/shard_map/dot_general | solution.py:120
  268.7 11.3 fusion.82
  280.0 4.7 all-to-all-start.1
  289.0 67.2 %all-to-all-done.1 = bf16[8,256,768]{2,1,0:T(8,128)(2,1)} async-done(((bf16[8,256,768]{2,1,0:T(8,128)(2,1)}), bf16[8,256,768]{2,1,0:T(8,128)(2,1)}, u32[]{:S(2)}, u32[]{:S(2)}) %all-to-all-start.1) | async-done | bytes 3145760 | tf_op jit(solution)/shard_map/all_to_all | solution.py:125
  356.2 7.9 gather_fusion
  364.1 2.6 copy.62
  366.7 3.9 multiply_convert_fusion.2
  370.6 2.6 copy.64
  373.2 7.9 scatter_custom_fusion.3
  381.0 76.2 %all_to_all.21 = bf16[8,256,768]{2,1,0:T(8,128)(2,1)} all-to-all(bf16[8,256,768]{2,1,0:T(8,128)(2,1)} %bitcast.179), channel_id=1, replica_groups=mesh['dp'=4,'expert'=8] {'expert'}, dimensions={0} | all-to-all | bytes 6291456 | tf_op jit(solution)/shard_map/all_to_all | solution.py:151
  457.3 32.7 %add_convert_fusion = bf16[2048,3072]{1,0:T(8,128)(2,1)} fusion(f32[2048,3072]{1,0:T(8,128)} %get-tuple-element.237, f32[2048,3072]{1,0:T(8,128)} %get-tuple-element.252, bf16[2048,768]{1,0:T(8,128)(2,1)} %bitcast.187, bf16[1,3072,768]{2,1,0:T(8,128)(2,1)} %param.37), kind=kOutput, calls=%fused_computation.71 | convolution fusion | flops 9751756800 | bytes 70778880 | tf_op jit(solution)/shard_map/rd,fd->rf/dot_general | solution.py:158
  489.9 15.5 %fusion.79 = bf16[2048,768]{1,0:T(8,128)(2,1)} fusion(bf16[2048,3072]{1,0:T(8,128)(2,1)} %add_convert_fusion, bf16[1,768,3072]{2,1,0:T(8,128)(2,1)} %param.36), kind=kOutput, calls=%fused_computation.110 | convolution fusion | flops 9665249280 | bytes 20447232 | tf_op jit(solution)/shard_map/rf,df->rd/dot_general | solution.py:167
  505.4 4.4 all-to-all-start.3
  510.4 71.0 %all-to-all-done.3 = bf16[8,256,768]{2,1,0:T(8,128)(2,1)} async-done(((bf16[8,256,768]{2,1,0:T(8,128)(2,1)}), bf16[8,256,768]{2,1,0:T(8,128)(2,1)}, u32[]{:S(2)}, u32[]{:S(2)}) %all-to-all-start.3) | async-done | bytes 3145760 | tf_op jit(solution)/shard_map/all_to_all | solution.py:170
  581.4 7.9 gather_fusion.1
  589.2 2.6 copy.65
  591.9 4.8 multiply_reduce_fusion.1
  597.5 3.9 fusion.121
  603.0 4.3 fusion.124
  608.8 2.8 copy.66
  615.6 150.9 %while.29 = (s32[]{:T(128)}, bf16[12,1,1024,64]{2,3,1,0:T(8,128)(2,1)}, bf16[12,1,1024,64]{2,3,1,0:T(8,128)(2,1)}, bf16[12,1,1024,64]{2,3,1,0:T(8,128)(2,1)}, bf...) while((s32[]{:T(128)}, ...), condition=%wide.region_23.24_spmd.clone, body=%wide.region_21.23_spmd.clone.sunk | while | flops 681901056 | bytes 33711208 | solution.py:215
  625.9 2.4 fusion.187
  634.0 2.4 fusion.186
  646.5 2.4 fusion.186
  659.1 2.4 fusion.186
  671.6 2.4 fusion.186
  676.1 2.4 fusion.187
  684.2 2.4 fusion.186
  709.3 2.4 fusion.186
  721.8 2.4 fusion.186
  734.4 2.4 fusion.186
  746.9 2.4 fusion.186
  759.5 2.4 fusion.186
  764.0 2.4 fusion.187
  766.6 4.6 fusion.111
  771.2 3.0 fusion.113
  774.2 3.0 fusion.115
  777.3 15.5 %fusion.76 = bf16[1,3072,768]{2,1,0:T(8,128)(2,1)} fusion(bf16[2048,3072]{1,0:T(8,128)(2,1)} %copy-done.51, bf16[2048,768]{1,0:T(8,128)(2,1)} %bitcast.188), kind=kOutput, calls=%fused_computation.105 | convolution fusion | flops 9666035712 | bytes 20447232 | tf_op jit(solution)/shard_map/rf,rd->fd/dot_general | solution.py:163
  792.9 14.6 %fusion.75 = bf16[1,768,3072]{2,1,0:T(8,128)(2,1)} fusion(bf16[2048,768]{1,0:T(8,128)(2,1)S(1)} %bitcast.186, bf16[2048,3072]{1,0:T(8,128)(2,1)} %add_convert_fusion), kind=kOutput, calls=%fused_computation.104 | convolution fusion | flops 9666035712 | bytes 20447232 | tf_op jit(solution)/shard_map/rd,rf->df/dot_general | solution.py:166
  807.7 165.0 %all-reduce.9.cloned.1.call-done = (f32[768,768]{1,0:T(8,128)}, f32[768,768]{1,0:T(8,128)}, f32[768,768]{1,0:T(8,128)}, f32[768,768]{1,0:T(8,128)}) async-done(((f32[768,768]{1,0:T(8,128)}, f32[768,768]{1,0:T(8,128)}, f32[768,768]{1,0:T(8,128)}, f32[768,768]{1,0:T(8,128)}), (f32[768,768]{1,0:T(8,128)}, f32[768,768]{1,0:T(8,128)}, f32[768,768]{1,0:T(8,128)}, ...) | async-done | bytes 9437200 | tf_op jit(solution)/shard_map/psum | solution.py:242
  972.8 3.3 fusion.125
  977.5 3.4 fusion.120
  984.0 3.5 add_convert_fusion.1
  987.4 2.7 copy.71
  991.7 27.1 %all-reduce = (f32[768]{0:T(1024)S(1)}, f32[768]{0:T(1024)S(1)}, f32[768]{0:T(1024)S(1)}, f32[768]{0:T(1024)S(1)}) all-reduce(f32[768]{0:T(1024)S(1)} %get-tuple-element.181, f32[768]{0:T(1024)S(1)} %get-tuple-element.184, f32[768]{0:T(1024)S(1)} %get-tuple-element.179, ...), channel_id=1, replica_groups=mesh['dp'=4,'expert'=8] {'expert'}, use_global_device_ids=true, to_apply=%region_27.28 | all-reduce | flops 3072 | bytes 24576 | tf_op jit(solution)/shard_map/psum | solution.py:242
  1018.8 17.0 %all-reduce.2 = (f32[768]{0:T(1024)}, f32[768]{0:T(1024)}, f32[768]{0:T(1024)}, f32[768]{0:T(1024)}) all-reduce(f32[768]{0:T(1024)S(1)} %get-tuple-element.216, f32[768]{0:T(1024)S(1)} %get-tuple-element.217, f32[768]{0:T(1024)S(1)} %get-tuple-element.218, f32[768]{0:T(1024)S(1)} %get-tuple-element.219), channel_id=1, replica_groups=mesh['dp'=4,'expert'=8] {'dp'}, use_global_device_ids=true, to_apply=%region_28.29 | all-reduce | flops 3072 | bytes 24576 | tf_op jit(solution)/shard_map/psum | solution.py:255
  1035.8 130.9 %all-reduce.13.cloned.1.call-done = (bf16[1,768,3072]{2,1,0:T(8,128)(2,1)}, bf16[1,3072,768]{2,1,0:T(8,128)(2,1)}) async-done(((bf16[1,768,3072]{2,1,0:T(8,128)(2,1)}, bf16[1,3072,768]{2,1,0:T(8,128)(2,1)}), (bf16[1,768,3072]{2,1,0:T(8,128)(2,1)}, bf16[1,3072,768]{2,1,0:T(8,128)(2,1)})) %all-reduce.13.cloned.1.call-update) | async-done | bytes 9437200 | tf_op jit(solution)/shard_map/psum | solution.py:239
  1166.7 7.5 broadcast_in_dim.122
  1174.3 4.9 broadcast_in_dim.124
  1179.2 181.8 %all-reduce.11.cloned.1.call-done = (f32[768,768]{1,0:T(8,128)}, f32[768,768]{1,0:T(8,128)}, f32[768,768]{1,0:T(8,128)}, f32[768,768]{1,0:T(8,128)}) async-done(((f32[768,768]{1,0:T(8,128)}, f32[768,768]{1,0:T(8,128)}, f32[768,768]{1,0:T(8,128)}, f32[768,768]{1,0:T(8,128)}), (f32[768,768]{1,0:T(8,128)}, f32[768,768]{1,0:T(8,128)}, f32[768,768]{1,0:T(8,128)}, ...) | async-done | bytes 9437200 | tf_op jit(solution)/shard_map/psum | solution.py:255
  1360.9 3.4 copy.116
  (279 shorter events, 216.2 us)
Async XLA Ops:
  7.2 10.6 copy-start
  7.2 3.2 copy-start.30
  7.2 3.2 copy-start.48
  9.0 87.7 %copy-start.1 = (bf16[1024,768]{0,1:T(8,128)(2,1)}, bf16[1024,768]{0,1:T(8,128)(2,1)S(1)}, u32[]{:S(2)}) copy-start(bf16[1024,768]{0,1:T(8,128)(2,1)S(1)} %copy.57) | copy-start | bytes 4718596
  9.0 1.8 copy-start.46
  9.3 15.3 %copy-start.23 = (f32[1024]{0:T(1024)}, f32[1024]{0:T(1024)S(1)}, u32[]{:S(2)}) copy-start(f32[1024]{0:T(1024)S(1)} %broadcast_multiply_fusion.1) | copy-start | bytes 12292
  9.8 0.6 copy-start.34
  10.9 13.7 copy-start.32
  100.0 1.7 copy-start.3
  100.0 2.1 copy-start.50
  100.0 2.3 copy-start.42
  100.0 7.4 copy-start.27
  100.1 7.4 copy-start.39
  100.1 7.4 copy-start.40
  100.1 12.5 copy-start.21
  102.1 0.6 copy-start.36
  102.1 10.5 copy-start.25
  119.2 86.1 %copy-start.41 = (s32[1024]{0:T(1024)}, s32[1024]{0:T(1024)S(1)}, u32[]{:S(2)}) copy-start(s32[1024]{0:T(1024)S(1)} %get-tuple-element.248) | copy-start | bytes 12292
  205.2 63.5 %copy-start.13 = (bf16[8,256,768]{2,1,0:T(8,128)(2,1)}, bf16[8,256,768]{2,1,0:T(8,128)(2,1)S(1)}, u32[]{:S(2)}) copy-start(bf16[8,256,768]{2,1,0:T(8,128)(2,1)S(1)} %all_to_all.20) | copy-start | bytes 9437188
  205.2 63.5 %copy-start.44 = (bf16[1,3072,768]{2,1,0:T(8,128)(2,1)S(1)}, bf16[1,3072,768]{2,1,0:T(8,128)(2,1)}, u32[]{:S(2)}) copy-start(bf16[1,3072,768]{2,1,0:T(8,128)(2,1)} %param.37) | copy-start | bytes 14155780
  268.7 11.3 copy-start.51
  280.0 76.2 %all-to-all-start.1 = ((bf16[8,256,768]{2,1,0:T(8,128)(2,1)}), bf16[8,256,768]{2,1,0:T(8,128)(2,1)}, u32[]{:S(2)}, u32[]{:S(2)}) async-start(bf16[8,256,768]{2,1,0:T(8,128)(2,1)} %bitcast.189), calls=%async_computation.1 | async-start | bytes 6291456 | tf_op jit(solution)/shard_map/all_to_all | solution.py:125
  284.7 2.4 copy-start.43
  284.7 4.3 copy-start.29
  284.7 71.5 %copy-start.38 = (s32[1024]{0:T(1024)S(1)}, s32[1024]{0:T(1024)}, u32[]{:S(2)}) copy-start(s32[1024]{0:T(1024)} %get-tuple-element.247) | copy-start | bytes 12292
  286.4 314.9 %copy-start.8 = (bf16[1024,768]{0,1:T(8,128)(2,1)}, bf16[1024,768]{0,1:T(8,128)(2,1)S(1)}, u32[]{:S(2)}) copy-start(bf16[1024,768]{0,1:T(8,128)(2,1)S(1)} %copy.63) | copy-start | bytes 4718596
  505.4 76.0 %all-to-all-start.3 = ((bf16[8,256,768]{2,1,0:T(8,128)(2,1)}), bf16[8,256,768]{2,1,0:T(8,128)(2,1)}, u32[]{:S(2)}, u32[]{:S(2)}) async-start(bf16[8,256,768]{2,1,0:T(8,128)(2,1)} %bitcast.190), calls=%async_computation.3 | async-start | bytes 6291456 | tf_op jit(solution)/shard_map/all_to_all | solution.py:170
  509.8 462.9 %all-reduce.9.cloned.1.call-start = ((), (), s32[]{:S(2)}) async-start(), calls=%async_computation.4 | async-start | bytes 18874368 | tf_op jit(solution)/shard_map/psum | solution.py:242
  589.2 2.6 copy-start.22
  589.2 2.6 copy-start.26
  589.2 2.6 copy-start.28
  591.9 4.9 copy-start.37
  591.9 4.9 copy-start.4
  591.9 5.1 copy-start.5
  591.9 5.6 copy-start.10
  601.4 1.6 copy-start.6
  603.0 4.4 copy-start.45
  615.6 150.9 %copy-start.2 = (bf16[1024,768]{0,1:T(8,128)(2,1)S(1)}, bf16[1024,768]{0,1:T(8,128)(2,1)}, u32[]{:S(2)}) copy-start(bf16[1024,768]{0,1:T(8,128)(2,1)} %copy-done.1) | copy-start | bytes 4718596
  615.6 150.9 %copy-start.24 = (f32[1024]{0:T(1024)S(1)}, f32[1024]{0:T(1024)}, u32[]{:S(2)}) copy-start(f32[1024]{0:T(1024)} %copy-done.23) | copy-start | bytes 12292
  615.6 150.9 %copy-start.31 = (f32[768]{0:T(1024)S(1)}, f32[768]{0:T(1024)}, u32[]{:S(2)}) copy-start(f32[768]{0:T(1024)} %param.27) | copy-start | bytes 9220
  615.6 151.0 %copy-start.33 = (f32[1024]{0:T(1024)S(1)}, f32[1024]{0:T(1024)}, u32[]{:S(2)}) copy-start(f32[1024]{0:T(1024)} %copy-done.32) | copy-start | bytes 12292
  615.6 151.0 %copy-start.49 = (f32[768]{0:T(1024)S(1)}, f32[768]{0:T(1024)}, u32[]{:S(2)}) copy-start(f32[768]{0:T(1024)} %param.28) | copy-start | bytes 9220
  766.6 4.6 copy-start.19
  771.1 3.0 copy-start.18
  777.3 389.5 %all-reduce.13.cloned.1.call-start = ((), (), s32[]{:S(2)}) async-start(), calls=%async_computation.6 | async-start | bytes 18874368 | tf_op jit(solution)/shard_map/psum | solution.py:239
  777.3 15.6 %copy-start.14 = (bf16[8,256,768]{2,1,0:T(8,128)(2,1)S(1)}, bf16[8,256,768]{2,1,0:T(8,128)(2,1)}, u32[]{:S(2)}) copy-start(bf16[8,256,768]{2,1,0:T(8,128)(2,1)} %copy-done.13) | copy-start | bytes 9437188
  807.4 553.5 %all-reduce.11.cloned.1.call-start = ((), (), s32[]{:S(2)}) async-start(), calls=%async_computation.5 | async-start | bytes 18874368 | tf_op jit(solution)/shard_map/psum | solution.py:255
  972.8 3.3 copy-start.20
  972.8 3.3 copy-start.47
  977.5 3.4 copy-start.35
  980.9 2.2 copy-start.7
  980.9 3.1 copy-start.9
  987.4 2.7 copy-start.11
  1166.7 7.5 copy-start.12
  1360.9 3.4 copy-start.17
  1364.3 2.5 copy-start.16
  1366.8 2.5 copy-start.15
Sparse Core Ops, SparseCore 0:
  777.4 195.3 all-reduce.8
  977.0 189.6 all-reduce.12
  1170.6 190.2 all-reduce.10
